TPU v7x, 256 devices: a whole 4x4x8 slice. The times are simulated.
256 devices in a mesh: dp: 32 (over x, z), seq: 8 (over y, core).
Axes of the slice: x: 4, y: 4, z: 8, core: 2. Of those that a mesh axis runs over, the one named last changes fastest.
Arguments:
- words: bfloat16 [128, 1024, 1024], P('dp', 'seq'), may hold values from -6 to 6
- patches: bfloat16 [128, 2048, 1024], P('dp', 'seq'), may hold values from -6 to 6
- proj: bfloat16 [1024, 1024], P('dp'), may hold values from -0.1875 to 0.1875
- routes: int32 [128, 1024, 1], P('dp', 'seq'), may hold values from 0 to 7; in each aligned block of 128 rows (0 to 127, 128 to 255, ..., all dimensions but the last counted through in order) at most 32 rows name the same one
- targets: int32 [128, 1024], P('dp', 'seq'), may hold values from 0 to 255
- counts: int32 [128], P('dp'), may hold values from 512 to 1024
- flags: int32 [128, 16, 32], P('dp'), may hold values 0 or 1
Outputs:
- word_loss: float32 [128, 1024], P('dp', 'seq')
- proj_grad: float32 [1024, 1024], P('dp', 'seq')
Inputs may be any that keep to these rules, and one draw needn't show every extreme that they name: `routes`: among the 128 words of one page held by one index of seq, at most 32 name the same shard; some block reaches 32.
All inputs are finite; a program needn't handle non-finite values. No bound on the sum of `flags` on one device may be relied on, other than what follows from the above.
Results may differ from a plain program's by a relative error of at most 0.0065.
Values may be sent and summed in bfloat16 or wider, within the bound.
A program may use at most 64 MiB of HBM per device.

v0:
```python
import math
import jax
import jax.numpy as jnp
from jax import lax
from jax.sharding import PartitionSpec as P

MARGIN_BLOCK_SIZE = 64


def local(words, patches, proj, routes, targets, counts, flags):
    pages, wdev, width = words.shape
    ppsz = patches.shape[1]
    nblk = flags.shape[1]
    nseq = lax.axis_size("seq")
    mine = lax.axis_index("seq")
    capacity_limit = 2 * wdev // nseq
    bps = ppsz // MARGIN_BLOCK_SIZE
    scale = 2.0 / math.sqrt(width)
    flat_rows = words.reshape(pages * wdev, width)
    columns = flat_rows
    query = jnp.dot(
        columns, lax.all_gather(proj, "dp", axis=0, tiled=True), preferred_element_type=jnp.float32
    )
    query = query.astype(jnp.bfloat16).reshape(pages, wdev, width)
    destination_slot = routes[:, :, 0]
    onehot = (
        destination_slot[:, :, None] == jnp.arange(nseq, dtype=jnp.int32)[None, None, :]
    ).astype(jnp.int32)
    rank = jnp.cumsum(onehot, axis=1) - onehot
    slot = jnp.sum(rank * onehot, axis=2)
    slot_hit = (
        slot[:, :, None] == jnp.arange(capacity_limit, dtype=jnp.int32)[None, None, :]
    ).astype(jnp.int32)
    dispatch = onehot[:, :, :, None] * slot_hit[:, :, None, :]
    dispatch_bf = dispatch.astype(jnp.bfloat16)
    word_idx = mine * wdev + jnp.arange(wdev, dtype=jnp.int32)
    q_buf = jnp.einsum(
        "pwhc,pwd->hpcd", dispatch_bf, query, preferred_element_type=jnp.float32
    ).astype(jnp.bfloat16)
    tgt_buf = jnp.einsum("pwhc,pw->hpc", dispatch, targets)
    idx_buf = jnp.einsum("pwhc,w->hpc", dispatch, word_idx + 1) - 1
    q_in, tgt_in, idx_in = (
        lax.all_to_all(q_buf, "seq", split_axis=0, concat_axis=0, tiled=True),
        lax.all_to_all(tgt_buf, "seq", split_axis=0, concat_axis=0, tiled=True),
        lax.all_to_all(idx_buf, "seq", split_axis=0, concat_axis=0, tiled=True),
    )
    scores = jnp.einsum("hpcd,pkd->hpck", q_in, patches, preferred_element_type=jnp.float32) * scale
    own = lax.dynamic_slice_in_dim(flags, mine * bps, bps, 2)
    word_block = jnp.maximum(idx_in, 0) // MARGIN_BLOCK_SIZE
    picked = (word_block[..., None] == jnp.arange(nblk, dtype=jnp.int32)).astype(jnp.int32)
    hit = jnp.sum(picked[..., None] * own[None, :, None, :, :], axis=-2)
    allowed = (hit > 0) | (
        (tgt_in // MARGIN_BLOCK_SIZE)[..., None] == jnp.arange(bps, dtype=jnp.int32)
    )
    mask = jnp.broadcast_to(allowed[..., None], allowed.shape + (MARGIN_BLOCK_SIZE,)).reshape(
        scores.shape
    )
    expo = jnp.where(mask, jnp.exp(scores), jnp.float32(0.0))
    total = jnp.sum(expo, axis=-1)
    is_target = jnp.arange(ppsz, dtype=jnp.int32) == tgt_in[..., None]
    target_score = jnp.sum(jnp.where(is_target, scores, jnp.float32(0.0)), axis=-1)
    valid_mask = (idx_in >= 0) & (idx_in < counts[None, :, None])
    loss_out = jnp.where(valid_mask, jnp.log(total) - target_score, jnp.float32(0.0))
    coef = jnp.where(
        valid_mask, jnp.float32(64.0) / counts.astype(jnp.float32)[None, :, None], jnp.float32(0.0)
    )
    dscore = (coef[..., None] * (expo / total[..., None] - is_target.astype(jnp.float32))).astype(
        jnp.bfloat16
    )
    dquery = (
        jnp.einsum("hpck,pkd->hpcd", dscore, patches, preferred_element_type=jnp.float32) * scale
    ).astype(jnp.bfloat16)
    loss_home = lax.all_to_all(loss_out, "seq", split_axis=0, concat_axis=0, tiled=True)
    dq_home = lax.all_to_all(dquery, "seq", split_axis=0, concat_axis=0, tiled=True)
    right = (
        jnp.einsum("pwhc,hpcd->pwd", dispatch_bf, dq_home, preferred_element_type=jnp.float32)
        .astype(jnp.bfloat16)
        .reshape(-1, width)
    )
    word_loss = jnp.einsum("pwhc,hpc->pw", dispatch.astype(jnp.float32), loss_home)
    columns = flat_rows
    partial_rows = lax.psum_scatter(
        jnp.einsum("rc,rd->cd", columns, right, preferred_element_type=jnp.float32),
        "dp",
        scatter_dimension=0,
        tiled=True,
    )
    proj_grad = lax.psum_scatter(partial_rows, "seq", scatter_dimension=1, tiled=True)
    return (word_loss, proj_grad)


def solution(mesh):
    in_specs = (
        P("dp", "seq", None),
        P("dp", "seq", None),
        P("dp", None),
        P("dp", "seq", None),
        P("dp", "seq"),
        P("dp"),
        P("dp", None, None),
    )
    out_specs = (P("dp", "seq"), P("dp", "seq"))
    return jax.shard_map(local, mesh=mesh, in_specs=in_specs, out_specs=out_specs, check_vma=False)
```

profile of v0, /device:TPU:4, one launch (start us, length us, event | category | flops | bytes accessed | tf_op | source)
XLA Modules:
  0.0 441.0 jit_solution(18329256724800153465)
XLA Ops:
  7.9 0.8 fusion.37
  9.1 0.9 select_reduce_fusion.1
  10.0 3.5 fusion.25
  14.2 4.5 %all-to-all-start = ((s32[8,1,128]{2,1,0:T(1,128)}), s32[8,1,128]{2,1,0:T(1,128)S(1)}, u32[]{:S(2)}, u32[]{:S(2)}) async-start(s32[8,1,128]{2,1,0:T(1,128)} %reshape.58), calls=%async_computation | async-start | bytes 8192 | tf_op jit(solution)/shard_map/all_to_all | solution.py:45
  18.7 4.2 fusion.23
  23.6 66.6 %all-gather.2.cloned.1.call-done = bf16[1024,1024]{1,0:T(8,128)(2,1)} async-done(((bf16[32,1024]{1,0:T(8,128)(2,1)}), bf16[1024,1024]{1,0:T(8,128)(2,1)}) %all-gather.2.cloned.1.call-update) | async-done | bytes 2097168 | tf_op jit(solution)/shard_map/all_gather | solution.py:22
  90.2 4.2 convolution_convert_fusion
  94.3 4.3 all-to-all-start.1
  98.6 3.3 convert_bitcast_fusion
  101.9 2.0 all-to-all-done.1
  103.9 4.4 all-to-all-start.2
  111.3 1.4 broadcast_in_dim.15
  113.5 21.9 %all-to-all-done.2 = bf16[8,4,32,1024]{3,2,1,0:T(8,128)(2,1)} async-done(((bf16[8,4,32,1024]{3,2,1,0:T(8,128)(2,1)}), bf16[8,4,32,1024]{3,2,1,0:T(8,128)(2,1)}, u32[]{:S(2)}, u32[]{:S(2)}) %all-to-all-start.2) | async-done | bytes 2097184 | tf_op jit(solution)/shard_map/all_to_all | solution.py:43
  135.4 2.7 fusion.27
  138.1 1.2 fusion.6
  139.3 30.8 %all_to_all.25 = bf16[8,4,32,1024]{3,2,1,0:T(8,128)(2,1)} all-to-all(bf16[8,4,32,1024]{3,2,1,0:T(8,128)(2,1)S(1)} %fusion.6), channel_id=1, replica_groups=mesh['dp'=32,'seq'=8] {'seq'}, dimensions={0} | all-to-all | bytes 4194304 | tf_op jit(solution)/shard_map/all_to_all | solution.py:74
  170.1 5.1 %convolution_bitcast_fusion = f32[1024,1024]{0,1:T(8,128)} fusion(bf16[4,128,1024]{2,1,0:T(8,128)(2,1)S(1)} %copy-done.1, bf16[8,4,32,1024]{3,2,1,0:T(8,128)(2,1)} %all_to_all.25, s32[4,128,32]{1,2,0:T(8,128)S(1)} %fusion.39, s32[4,128,8]{1,2,0:T(8,128)S(1)} %copy.34), kind=kOutput, calls=%fused_computation.1 | convolution fusion | flops 1342963712 | bytes 7421952 | tf_op jit(solution)/shard_map/rc,rd->cd/dot_general | solution.py:83
  175.2 5.3 %copy.63 = f32[1024,1024]{1,0:T(8,128)} copy(f32[1024,1024]{0,1:T(8,128)} %convolution_bitcast_fusion) | data formatting | bytes 8388608
  180.7 216.9 %reduce-scatter.7.cloned.1.call-done = f32[32,1024]{1,0:T(8,128)} async-done(((f32[1024,1024]{1,0:T(8,128)}), f32[32,1024]{1,0:T(8,128)}) %reduce-scatter.7.cloned.1.call-update) | async-done | bytes 131088
  397.6 1.9 copy.64
  399.5 9.4 %all_to_all.26 = bf16[8,4,32]{2,1,0:T(4,128)(2,1)S(1)} all-to-all(bf16[8,4,32]{2,1,0:T(4,128)(2,1)S(1)} %copy.49), channel_id=1, replica_groups=mesh['dp'=32,'seq'=8] {'seq'}, dimensions={0} | all-to-all | bytes 4096 | tf_op jit(solution)/shard_map/all_to_all | solution.py:73
  408.9 0.8 fusion.28
  409.7 23.2 %reduce-scatter.5.cloned.1.call-done = f32[32,128]{0,1:T(8,128)} async-done(((f32[32,1024]{0,1:T(8,128)}), f32[32,128]{0,1:T(8,128)}) %reduce-scatter.5.cloned.1.call-update) | async-done | bytes 16400 | tf_op jit(solution)/shard_map/reduce_scatter | solution.py:88
  432.9 1.5 copy.53
  (42 shorter events, 6.4 us)
Async XLA Ops:
  7.2 128.3 %copy-start = (bf16[4,256,1024]{2,1,0:T(8,128)(2,1)S(1)}, bf16[4,256,1024]{2,1,0:T(8,128)(2,1)}, u32[]{:S(2)}) copy-start(bf16[4,256,1024]{2,1,0:T(8,128)(2,1)} %param.8) | copy-start | bytes 6291460
  7.2 83.0 %all-gather.2.cloned.1.call-start = ((), (), s32[]{:S(2)}) async-start(), calls=%async_computation.7 | async-start | bytes 2162688 | tf_op jit(solution)/shard_map/all_gather | solution.py:22
  14.2 80.1 %all-to-all-start = ((s32[8,1,128]{2,1,0:T(1,128)}), s32[8,1,128]{2,1,0:T(1,128)S(1)}, u32[]{:S(2)}, u32[]{:S(2)}) async-start(s32[8,1,128]{2,1,0:T(1,128)} %reshape.58), calls=%async_computation | async-start | bytes 8192 | tf_op jit(solution)/shard_map/all_to_all | solution.py:45
  94.3 9.5 %all-to-all-start.1 = ((s32[8,1,128]{2,1,0:T(1,128)}), s32[8,1,128]{2,1,0:T(1,128)S(1)}, u32[]{:S(2)}, u32[]{:S(2)}) async-start(s32[8,1,128]{2,1,0:T(1,128)} %reshape.60), calls=%async_computation.1 | async-start | bytes 8192 | tf_op jit(solution)/shard_map/all_to_all | solution.py:44
  101.9 6.4 %copy-start.2 = (s32[4,16,32]{2,1,0:T(8,128)S(1)}, s32[4,16,32]{2,1,0:T(8,128)}, u32[]{:S(2)}) copy-start(s32[4,16,32]{2,1,0:T(8,128)} %param.13) | copy-start | bytes 24580
  101.9 6.6 %copy-start.3 = (s32[4]{0:T(128)S(1)}, s32[4]{0:T(128)}, u32[]{:S(2)}) copy-start(s32[4]{0:T(128)} %param.12) | copy-start | bytes 52
  103.9 31.6 %all-to-all-start.2 = ((bf16[8,4,32,1024]{3,2,1,0:T(8,128)(2,1)}), bf16[8,4,32,1024]{3,2,1,0:T(8,128)(2,1)}, u32[]{:S(2)}, u32[]{:S(2)}) async-start(bf16[8,4,32,1024]{3,2,1,0:T(8,128)(2,1)} %convert_bitcast_fusion), calls=%async_computation.2 | async-start | bytes 4194304 | tf_op jit(solution)/shard_map/all_to_all | solution.py:43
  108.2 289.3 %reduce-scatter.7.cloned.1.call-start = ((), (), s32[]{:S(2)}) async-start(), calls=%async_computation.9 | async-start | bytes 4325376
  139.3 30.8 %copy-start.1 = (bf16[4,128,1024]{2,1,0:T(8,128)(2,1)S(1)}, bf16[4,128,1024]{2,1,0:T(8,128)(2,1)}, u32[]{:S(2)}) copy-start(bf16[4,128,1024]{2,1,0:T(8,128)(2,1)} %param.7) | copy-start | bytes 3145732
  180.6 252.3 %reduce-scatter.5.cloned.1.call-start = ((), (), s32[]{:S(2)}) async-start(), calls=%async_computation.8 | async-start | bytes 589824 | tf_op jit(solution)/shard_map/reduce_scatter | solution.py:88
Sparse Core Ops, SparseCore 0:
  10.6 79.5 all-gather.1
  180.7 216.7 reduce-scatter.6
  400.2 32.6 reduce-scatter.4
where the time goes:
time: 442 us; the launch traced here: 441 us
  waiting for transfers between devices  331 us (75%)
  blocking collectives  40.2 us (9%)
  matrix products  24.9 us (6%)
  between operations  13.9 us (3%)
  local copies, waits for them, and re-layouts  13.6 us (3%)
  starting transfers between devices  13.3 us (3%)
    unnamed x4, waiting for transfers between devices  218 us
    all_gather x1, waiting for transfers between devices, local(): lax.all_gather(proj, 'dp', axis=0, tiled=True)  66.6 us
    all_to_all x1, blocking collectives, local(): lax.all_to_all(dquery, 'seq', split_axis=0, concat_axis=0, tiled=True)  30.8 us
    reduce_scatter x1, waiting for transfers between devices, local(): lax.psum_scatter(partial_rows, 'seq', scatter_dimension=1, tiled=True)  23.2 us
    all_to_all x1, waiting for transfers between devices, local(): lax.all_to_all(q_buf, 'seq', split_axis=0, concat_axis=0, tiled=True)  21.9 us
    unnamed x15, local copies, waits for them, and re-layouts  10.3 us
    all_to_all x1, blocking collectives, local(): lax.all_to_all(loss_out, 'seq', split_axis=0, concat_axis=0, tiled=True)  9.4 us
  transfers between devices with their start and end apart: 6, of which 5 were waited for; matrix products, arithmetic and copies ran while one was open for 6% of the time, Pallas kernels for 0%

commit v1 on v0

--- a/solution.py
+++ b/solution.py
@@ -3,6 +3,7 @@
 import jax.numpy as jnp
 from jax import lax
 from jax.sharding import PartitionSpec as P
+from jax.lax import all_to_all, axis_size
 
 MARGIN_BLOCK_SIZE = 64
 
@@ -18,9 +19,10 @@
     scale = 2.0 / math.sqrt(width)
     flat_rows = words.reshape(pages * wdev, width)
     columns = flat_rows
-    query = jnp.dot(
-        columns, lax.all_gather(proj, "dp", axis=0, tiled=True), preferred_element_type=jnp.float32
+    manage_trees_all = lambda field_in, axis_id: jnp.concatenate(
+        all_to_all(jnp.stack([field_in] * axis_size(axis_id), axis=0), axis_id, 0, 0), axis=0
     )
+    query = jnp.dot(columns, manage_trees_all(proj, "dp"), preferred_element_type=jnp.float32)
     query = query.astype(jnp.bfloat16).reshape(pages, wdev, width)
     destination_slot = routes[:, :, 0]
     onehot = (

time: 442 us -> 427 us (0.966)
  waiting for transfers between devices: 331 us -> 304 us
  starting transfers between devices: 13.3 us -> 24.2 us
    all_gather x1 -> x0, waiting for transfers between devices: 66.6 us -> none  [local(): lax.all_gather(proj, 'dp', axis=0, tiled=True)]
    all_to_all x0 -> x1, waiting for transfers between devices: none -> 36.8 us  [local(): all_to_all(jnp.stack([field_in] * axis_size(axis_id), axis=0), axis_id, 0...]
    all_to_all x0 -> x1, starting transfers between devices: none -> 11.8 us  [local(): all_to_all(jnp.stack([field_in] * axis_size(axis_id), axis=0), axis_id, 0...]
    unnamed x4 -> x3, waiting for transfers between devices: 218 us -> 218 us
    unnamed x15 -> x21, local copies, waits for them, and re-layouts: 10.3 us -> 10.3 us
  transfers between devices with their start and end apart: 6 -> 6, of which waited for: 5 -> 6; matrix products, arithmetic and copies ran while one was open for 6% -> 6% of each run, Pallas kernels for 0% -> 0%
where the time goes in v1:
time: 427 us; the launch traced here: 426 us
  waiting for transfers between devices  304 us (71%)
  blocking collectives  40.1 us (9%)
  starting transfers between devices  24.2 us (6%)
  matrix products  23.8 us (6%)
  local copies, waits for them, and re-layouts  16.2 us (4%)
  between operations  14.2 us (3%)
    unnamed x3, waiting for transfers between devices  218 us
    all_to_all x1, waiting for transfers between devices, local(): all_to_all(jnp.stack([field_in] * axis_size(axis_id), axis=0), axis_id, 0...  36.8 us
    all_to_all x1, blocking collectives, local(): lax.all_to_all(dquery, 'seq', split_axis=0, concat_axis=0, tiled=True)  30.8 us
    reduce_scatter x1, waiting for transfers between devices, local(): lax.psum_scatter(partial_rows, 'seq', scatter_dimension=1, tiled=True)  23.2 us
    all_to_all x1, waiting for transfers between devices, local(): lax.all_to_all(q_buf, 'seq', split_axis=0, concat_axis=0, tiled=True)  21.9 us
    all_to_all x1, starting transfers between devices, local(): all_to_all(jnp.stack([field_in] * axis_size(axis_id), axis=0), axis_id, 0...  11.8 us
    unnamed x21, local copies, waits for them, and re-layouts  10.3 us
    all_to_all x1, blocking collectives, local(): lax.all_to_all(loss_out, 'seq', split_axis=0, concat_axis=0, tiled=True)  9.34 us
  transfers between devices with their start and end apart: 6, of which 6 were waited for; matrix products, arithmetic and copies ran while one was open for 6% of the time, Pallas kernels for 0%

profile of v1, /device:TPU:4, one launch (start us, length us, event | category | flops | bytes accessed | tf_op | source)
XLA Modules:
  0.0 426.3 jit_solution(423757124714431418)
XLA Ops:
  7.2 2.5 stack.2
  9.7 11.8 %all-to-all-start.2 = ((bf16[32,32,1024]{2,1,0:T(8,128)(2,1)}), bf16[32,32,1024]{2,1,0:T(8,128)(2,1)}, u32[]{:S(2)}, u32[]{:S(2)}) async-start(bf16[32,32,1024]{2,1,0:T(8,128)(2,1)} %stack.2), calls=%async_computation.2 | async-start | bytes 4194304 | tf_op jit(solution)/shard_map/all_to_all | solution.py:23
  23.9 3.5 fusion.25
  28.1 3.5 fusion.23
  32.3 36.8 %all-to-all-done.2 = bf16[32,32,1024]{2,1,0:T(8,128)(2,1)} async-done(((bf16[32,32,1024]{2,1,0:T(8,128)(2,1)}), bf16[32,32,1024]{2,1,0:T(8,128)(2,1)}, u32[]{:S(2)}, u32[]{:S(2)}) %all-to-all-start.2) | async-done | bytes 2097184 | tf_op jit(solution)/shard_map/all_to_all | solution.py:23
  69.1 4.5 %all-to-all-start = ((s32[8,1,128]{2,1,0:T(1,128)}), s32[8,1,128]{2,1,0:T(1,128)S(1)}, u32[]{:S(2)}, u32[]{:S(2)}) async-start(s32[8,1,128]{2,1,0:T(1,128)} %reshape.64), calls=%async_computation | async-start | bytes 8192 | tf_op jit(solution)/shard_map/all_to_all | solution.py:47
  73.6 3.8 convolution_convert_fusion
  77.4 1.4 all-to-all-done
  78.8 3.4 all-to-all-start.1
  82.2 3.3 convert_bitcast_fusion
  85.5 2.0 all-to-all-done.1
  87.5 4.4 %all-to-all-start.3 = ((bf16[8,4,32,1024]{3,2,1,0:T(8,128)(2,1)}), bf16[8,4,32,1024]{3,2,1,0:T(8,128)(2,1)}, u32[]{:S(2)}, u32[]{:S(2)}) async-start(bf16[8,4,32,1024]{3,2,1,0:T(8,128)(2,1)} %convert_bitcast_fusion), calls=%async_computation.3 | async-start | bytes 4194304 | tf_op jit(solution)/shard_map/all_to_all | solution.py:45
  94.9 1.4 broadcast_in_dim.15
  97.1 21.9 %all-to-all-done.3 = bf16[8,4,32,1024]{3,2,1,0:T(8,128)(2,1)} async-done(((bf16[8,4,32,1024]{3,2,1,0:T(8,128)(2,1)}), bf16[8,4,32,1024]{3,2,1,0:T(8,128)(2,1)}, u32[]{:S(2)}, u32[]{:S(2)}) %all-to-all-start.3) | async-done | bytes 2097184 | tf_op jit(solution)/shard_map/all_to_all | solution.py:45
  119.0 2.7 fusion.27
  121.7 1.2 fusion.6
  122.9 30.8 %all_to_all.30 = bf16[8,4,32,1024]{3,2,1,0:T(8,128)(2,1)} all-to-all(bf16[8,4,32,1024]{3,2,1,0:T(8,128)(2,1)S(1)} %fusion.6), channel_id=1, replica_groups=mesh['dp'=32,'seq'=8] {'seq'}, dimensions={0} | all-to-all | bytes 4194304 | tf_op jit(solution)/shard_map/all_to_all | solution.py:76
  153.7 5.1 %convolution_bitcast_fusion = f32[1024,1024]{0,1:T(8,128)} fusion(bf16[4,128,1024]{2,1,0:T(8,128)(2,1)S(1)} %copy-done.2, bf16[8,4,32,1024]{3,2,1,0:T(8,128)(2,1)} %all_to_all.30, s32[4,128,32]{1,2,0:T(8,128)S(1)} %fusion.39, s32[4,128,8]{1,2,0:T(8,128)S(1)} %copy.34), kind=kOutput, calls=%fused_computation.1 | convolution fusion | flops 1342963712 | bytes 7421952 | tf_op jit(solution)/shard_map/rc,rd->cd/dot_general | solution.py:85
  158.9 5.3 %copy.63 = f32[1024,1024]{1,0:T(8,128)} copy(f32[1024,1024]{0,1:T(8,128)} %convolution_bitcast_fusion) | data formatting | bytes 8388608
  164.3 218.4 %reduce-scatter.7.cloned.1.call-done = f32[32,1024]{1,0:T(8,128)} async-done(((f32[1024,1024]{1,0:T(8,128)}), f32[32,1024]{1,0:T(8,128)}) %reduce-scatter.7.cloned.1.call-update) | async-done | bytes 131088
  382.7 1.9 copy.64
  384.6 9.3 %all_to_all.31 = bf16[8,4,32]{2,1,0:T(4,128)(2,1)S(1)} all-to-all(bf16[8,4,32]{2,1,0:T(4,128)(2,1)S(1)} %copy.49), channel_id=1, replica_groups=mesh['dp'=32,'seq'=8] {'seq'}, dimensions={0} | all-to-all | bytes 4096 | tf_op jit(solution)/shard_map/all_to_all | solution.py:75
  394.8 23.2 %reduce-scatter.5.cloned.1.call-done = f32[32,128]{0,1:T(8,128)} async-done(((f32[32,1024]{0,1:T(8,128)}), f32[32,128]{0,1:T(8,128)}) %reduce-scatter.5.cloned.1.call-update) | async-done | bytes 16400 | tf_op jit(solution)/shard_map/reduce_scatter | solution.py:90
  418.0 1.5 copy.53
  (48 shorter events, 8.5 us)
Async XLA Ops:
  7.2 111.9 %copy-start = (bf16[4,256,1024]{2,1,0:T(8,128)(2,1)S(1)}, bf16[4,256,1024]{2,1,0:T(8,128)(2,1)}, u32[]{:S(2)}) copy-start(bf16[4,256,1024]{2,1,0:T(8,128)(2,1)} %param.8) | copy-start | bytes 6291460
  9.7 11.8 %copy-start.4 = (s32[4,128,1]{1,2,0:T(1,128)S(1)}, s32[4,128,1]{1,2,0:T(1,128)}, u32[]{:S(2)}) copy-start(s32[4,128,1]{1,2,0:T(1,128)} %param.10) | copy-start | bytes 6148
  9.7 18.4 %copy-start.6 = (s32[4,128]{1,0:T(4,128)S(1)}, s32[4,128]{1,0:T(4,128)}, u32[]{:S(2)}) copy-start(s32[4,128]{1,0:T(4,128)} %param.11) | copy-start | bytes 6148
  9.7 63.8 %copy-start.1 = (bf16[4,128,1024]{2,1,0:T(8,128)(2,1)S(1)}, bf16[4,128,1024]{2,1,0:T(8,128)(2,1)}, u32[]{:S(2)}) copy-start(bf16[4,128,1024]{2,1,0:T(8,128)(2,1)} %param.7) | copy-start | bytes 3145732
  9.7 59.4 %all-to-all-start.2 = ((bf16[32,32,1024]{2,1,0:T(8,128)(2,1)}), bf16[32,32,1024]{2,1,0:T(8,128)(2,1)}, u32[]{:S(2)}, u32[]{:S(2)}) async-start(bf16[32,32,1024]{2,1,0:T(8,128)(2,1)} %stack.2), calls=%async_computation.2 | async-start | bytes 4194304 | tf_op jit(solution)/shard_map/all_to_all | solution.py:23
  69.1 9.7 %all-to-all-start = ((s32[8,1,128]{2,1,0:T(1,128)}), s32[8,1,128]{2,1,0:T(1,128)S(1)}, u32[]{:S(2)}, u32[]{:S(2)}) async-start(s32[8,1,128]{2,1,0:T(1,128)} %reshape.64), calls=%async_computation | async-start | bytes 8192 | tf_op jit(solution)/shard_map/all_to_all | solution.py:47
  78.8 8.7 %all-to-all-start.1 = ((s32[8,1,128]{2,1,0:T(1,128)}), s32[8,1,128]{2,1,0:T(1,128)S(1)}, u32[]{:S(2)}, u32[]{:S(2)}) async-start(s32[8,1,128]{2,1,0:T(1,128)} %reshape.66), calls=%async_computation.1 | async-start | bytes 8192 | tf_op jit(solution)/shard_map/all_to_all | solution.py:46
  85.5 6.4 %copy-start.3 = (s32[4,16,32]{2,1,0:T(8,128)S(1)}, s32[4,16,32]{2,1,0:T(8,128)}, u32[]{:S(2)}) copy-start(s32[4,16,32]{2,1,0:T(8,128)} %param.13) | copy-start | bytes 24580
  85.5 6.6 %copy-start.5 = (s32[4]{0:T(128)S(1)}, s32[4]{0:T(128)}, u32[]{:S(2)}) copy-start(s32[4]{0:T(128)} %param.12) | copy-start | bytes 52
  87.5 31.6 %all-to-all-start.3 = ((bf16[8,4,32,1024]{3,2,1,0:T(8,128)(2,1)}), bf16[8,4,32,1024]{3,2,1,0:T(8,128)(2,1)}, u32[]{:S(2)}, u32[]{:S(2)}) async-start(bf16[8,4,32,1024]{3,2,1,0:T(8,128)(2,1)} %convert_bitcast_fusion), calls=%async_computation.3 | async-start | bytes 4194304 | tf_op jit(solution)/shard_map/all_to_all | solution.py:45
  91.8 290.8 %reduce-scatter.7.cloned.1.call-start = ((), (), s32[]{:S(2)}) async-start(), calls=%async_computation.9 | async-start | bytes 4325376
  122.9 30.8 %copy-start.2 = (bf16[4,128,1024]{2,1,0:T(8,128)(2,1)S(1)}, bf16[4,128,1024]{2,1,0:T(8,128)(2,1)}, u32[]{:S(2)}) copy-start(bf16[4,128,1024]{2,1,0:T(8,128)(2,1)} %param.7) | copy-start | bytes 3145732
  164.2 253.7 %reduce-scatter.5.cloned.1.call-start = ((), (), s32[]{:S(2)}) async-start(), calls=%async_computation.8 | async-start | bytes 589824 | tf_op jit(solution)/shard_map/reduce_scatter | solution.py:90
Sparse Core Ops, SparseCore 0:
  164.3 218.2 reduce-scatter.6
  385.3 32.5 reduce-scatter.4
